TPU v7x, 128 devices: a whole 4x4x4 slice. The times are simulated.
128 devices in a mesh: req: 32 (over y, x, core), mlp: 4 (over z).
Axes of the slice: x: 4, y: 4, z: 4, core: 2. Of those that a mesh axis runs over, the one named last changes fastest.
Arguments:
- tokens: bfloat16 [8192, 2560], P('req'), may hold values from -125 to 125
- lengths: int32 [32, 4], P('req'), may hold values from 1 to 128, 256 in all within a row
- page_table: int32 [32, 16], P('req'), may hold values from 0 to 15, each once within a row
- attn_norm: float32 [2560], replicated, may hold values from 0.25 to 1.75
- qkv_weight: bfloat16 [2560, 8, 768], P(None, 'mlp'), may hold values from -0.125 to 0.125
- q_norm: float32 [128], replicated, may hold values from 0.25 to 1.75
- k_norm: float32 [128], replicated, may hold values from 0.25 to 1.75
- o_weight: bfloat16 [4096, 2560], P('mlp'), may hold values from -0.09375 to 0.09375
- mlp_norm: float32 [2560], replicated, may hold values from 0.25 to 1.75
- gate_up: bfloat16 [9728, 2, 2560], P(('req', 'mlp')), may hold values from -0.125 to 0.125
- down_weight: bfloat16 [9728, 2560], P(('req', 'mlp')), may hold values from -0.0625 to 0.0625
Outputs:
- layer_out: bfloat16 [8192, 2560], P(('req', 'mlp'))
- kv_cache: bfloat16 [2, 512, 16, 8, 128], P(None, 'req', None, 'mlp')
Inputs may be any that keep to these rules, and one draw needn't show every extreme that they name: `lengths`: each row sums to 256, and the longest prompt of every pack is exactly 128. `page_table`: each row is a permutation of 0 .. 15.
All inputs are finite; a program needn't handle non-finite values.
Results may differ from a plain program's by a relative error of at most 0.0049.
Values may be sent and summed in bfloat16 or wider, within the bound.
No kernel may reach another device: no remote copies, remote signals or barrier semaphores. Data moves between devices by JAX's collectives and lax.ppermute only.
A program may use at most 128 MiB of HBM per device.

v0:
```python
import math
import jax
import jax.numpy as jnp
from jax import lax
from jax.sharding import PartitionSpec as P

rope_theta = 1000000.0
norm_eps = 1e-06


def rms_scale(values, gain):
    mean_sq = jnp.mean(values * values, axis=-1, keepdims=True)
    return values * lax.rsqrt(mean_sq + norm_eps) * gain


def positions_of(lengths, slots):
    ends = jnp.cumsum(lengths)
    slot_ids = jnp.arange(slots, dtype=jnp.int32)
    passed = (ends[None, :] <= slot_ids[:, None]).astype(jnp.int32)
    segment = jnp.sum(passed, axis=1)
    start = jnp.sum(passed * lengths[None, :], axis=1)
    return (slot_ids, segment, slot_ids - start)


def rotate(values, position, head_dim):
    half = head_dim // 2
    freq = rope_theta ** (-(2.0 * jnp.arange(half, dtype=jnp.float32)) / head_dim)
    angle = position.astype(jnp.float32)[:, None] * freq[None, :]
    shape = (angle.shape[0],) + (1,) * (values.ndim - 2) + (half,)
    cosine = jnp.cos(angle).reshape(shape)
    sine = jnp.sin(angle).reshape(shape)
    first = values[..., :half]
    second = values[..., half:]
    return jnp.concatenate(
        [first * cosine - second * sine, second * cosine + first * sine], axis=-1
    )


def feed_forward(rows, unit_pairs, unit_down):
    gate = jnp.einsum("td,fd->tf", rows, unit_pairs[:, 0, :], preferred_element_type=jnp.float32)
    upper = jnp.einsum("td,fd->tf", rows, unit_pairs[:, 1, :], preferred_element_type=jnp.float32)
    act = (jax.nn.silu(gate) * upper).astype(jnp.bfloat16)
    return jnp.dot(act, unit_down, preferred_element_type=jnp.float32)


def per_device(
    tokens,
    lengths,
    page_table,
    attn_norm,
    qkv_weight,
    q_norm,
    k_norm,
    o_weight,
    mlp_norm,
    gate_up,
    down_weight,
):
    slots = tokens.shape[0]
    head_dim = q_norm.shape[0]
    local_kv = qkv_weight.shape[1]
    group_q = qkv_weight.shape[2] // head_dim - 2
    pages = page_table.shape[1]
    page_rows = slots // pages
    owned = slots // lax.axis_size("mlp")
    slot_ids, segment, position = positions_of(lengths[0], slots)
    normed = rms_scale(tokens.astype(jnp.float32), attn_norm).astype(jnp.bfloat16)
    qkv = jnp.einsum("sd,dkc->skc", normed, qkv_weight, preferred_element_type=jnp.float32)
    query = qkv[:, :, : group_q * head_dim].reshape(slots, local_kv, group_q, head_dim)
    key = qkv[:, :, group_q * head_dim : (group_q + 1) * head_dim]
    value = qkv[:, :, (group_q + 1) * head_dim :]
    query = rotate(rms_scale(query, q_norm), position, head_dim).astype(jnp.bfloat16)
    key = rotate(rms_scale(key, k_norm), position, head_dim).astype(jnp.bfloat16)
    value = value.astype(jnp.bfloat16)
    key_pages = key.reshape(pages, page_rows, local_kv, head_dim)
    value_pages = value.reshape(pages, page_rows, local_kv, head_dim)
    kv_cache = jnp.zeros((2, pages, page_rows, local_kv, head_dim), jnp.bfloat16)
    kv_cache = kv_cache.at[:, page_table[0]].set(jnp.stack([key_pages, value_pages]))
    scores = jnp.einsum(
        "skgd,tkd->kgst", query, key, preferred_element_type=jnp.float32
    ) / math.sqrt(head_dim)
    allowed = (segment[:, None] == segment[None, :]) & (slot_ids[None, :] <= slot_ids[:, None])
    weights = jnp.where(allowed, jnp.exp(scores), 0.0)
    probs = (weights / jnp.sum(weights, axis=-1, keepdims=True)).astype(jnp.bfloat16)
    context = jnp.einsum("kgst,tkd->skgd", probs, value, preferred_element_type=jnp.float32)
    context = context.astype(jnp.bfloat16).reshape(slots, local_kv * group_q * head_dim)
    piece = context
    attn_out = lax.psum_scatter(
        jnp.dot(piece, o_weight, preferred_element_type=jnp.float32),
        "mlp",
        scatter_dimension=0,
        tiled=True,
    )
    mine = lax.dynamic_slice_in_dim(tokens, lax.axis_index("mlp") * owned, owned, 0).astype(
        jnp.float32
    )
    resid = mine + attn_out
    mlp_in = rms_scale(resid, mlp_norm).astype(jnp.bfloat16)
    unit_pairs, unit_down = (
        lax.all_gather(gate_up, "mlp", axis=0, tiled=True),
        lax.all_gather(down_weight, "mlp", axis=0, tiled=True),
    )
    gathered = lax.all_gather(mlp_in, "req", axis=0, tiled=True)
    piece = gathered
    mlp_out = lax.psum_scatter(
        feed_forward(piece, unit_pairs, unit_down).astype(jnp.bfloat16),
        "req",
        scatter_dimension=0,
        tiled=True,
    ).astype(jnp.float32)
    layer_out = (resid + mlp_out).astype(jnp.bfloat16)
    return (layer_out, kv_cache)


def solution(mesh):
    return jax.shard_map(
        per_device,
        mesh=mesh,
        in_specs=(
            P("req", None),
            P("req", None),
            P("req", None),
            P(),
            P(None, "mlp", None),
            P(),
            P(),
            P("mlp", None),
            P(),
            P(("req", "mlp"), None, None),
            P(("req", "mlp"), None),
        ),
        out_specs=(P(("req", "mlp"), None), P(None, "req", None, "mlp", None)),
        check_vma=False,
    )
```

profile of v0, /device:TPU:0, one launch (start us, length us, event | category | flops | bytes accessed | tf_op | source)
XLA Modules:
  0.0 324.5 jit_solution(15002400929183191970)
XLA Ops:
  7.2 0.0 reduce-scatter.3.cloned.1.call-start
  7.2 1.7 fusion.3
  8.9 5.9 %fusion = f32[256,2,768]{2,0,1:T(8,128)S(1)} fusion(bf16[2560,2,768]{2,1,0:T(2,128)(2,1)} %param.15, bf16[256,2560]{1,0:T(8,128)(2,1)} %param.11, f32[2560]{0:T(1024)} %param.14, f32[256]{0:T(256)S(1)} %add_rsqrt_fusion.2), kind=kOutput, calls=%fused_computation.2 | convolution fusion | flops 2015887360 | bytes 10759168 | tf_op jit(solution)/shard_map/sd,dkc->skc/dot_general | solution.py:68
  14.8 0.1 multiply_reduce_fusion.2
  15.0 1.0 copy-done.2
  16.0 0.3 fusion.28
  16.2 0.2 reduce-window.8
  16.4 0.1 convert_reduce_fusion
  16.5 0.1 fusion.18
  16.7 0.4 reshape.246
  17.0 0.6 multiply_reduce_fusion
  17.6 0.1 copy.53
  17.8 0.5 multiply_cosine_fusion
  18.3 1.1 multiply_multiply_fusion
  19.4 0.2 subtract_convert_fusion.1
  19.6 0.3 fusion.12
  19.9 0.4 subtract_convert_fusion
  20.4 0.8 fusion.6
  21.2 0.0 slice-start
  21.3 1.7 convolution_convert_fusion.1
  23.0 0.5 slice-done
  23.5 0.3 slice-done.1
  23.8 3.1 fusion.30
  26.9 0.0 reduce-scatter.3.cloned.1.call-update
  26.9 0.0 all-gather.9.cloned.1.call-start
  26.9 0.7 all-gather.9.cloned.1.call-update
  27.6 0.0 all-gather.7.cloned.1.call-start
  27.7 0.7 all-gather.7.cloned.1.call-update
  28.4 0.0 all-gather.5.cloned.1.call-start
  28.4 35.3 %reduce-scatter.3.cloned.1.call-done = f32[64,2560]{1,0:T(8,128)} async-done(((f32[256,2560]{1,0:T(8,128)}), f32[64,2560]{1,0:T(8,128)}) %reduce-scatter.3.cloned.1.call-update) | async-done | bytes 655376 | tf_op jit(solution)/shard_map/reduce_scatter | solution.py:88
  63.8 1.3 multiply_reduce_fusion.1
  65.1 1.9 multiply_convert_fusion
  67.0 0.0 all-gather.5.cloned.1.call-update
  67.0 0.2 reduce-scatter.5.cloned.1.call-start
  67.3 25.0 %all-gather.9.cloned.1.call-done = bf16[4,76,2560]{2,1,0:T(8,128)(2,1)} async-done(((bf16[1,76,2560]{2,1,0:T(8,128)(2,1)}), bf16[4,76,2560]{2,1,0:T(8,128)(2,1)}) %all-gather.9.cloned.1.call-update) | async-done | bytes 1556496 | tf_op jit(solution)/shard_map/all_gather | solution.py:101
  92.2 1.6 reshape.257
  93.8 39.3 %all-gather.7.cloned.1.call-done = bf16[304,2,2560]{2,1,0:T(2,128)(2,1)} async-done(((bf16[76,2,2560]{2,1,0:T(2,128)(2,1)}), bf16[304,2,2560]{2,1,0:T(2,128)(2,1)}) %all-gather.7.cloned.1.call-update) | async-done | bytes 3112976 | tf_op jit(solution)/shard_map/all_gather | solution.py:100
  133.1 9.4 %fusion.27 = (bf16[304,1,2560]{2,1,0:T(2,128)(2,1)}, bf16[304,1,2560]{2,1,0:T(2,128)(2,1)}) fusion(bf16[304,2,2560]{2,1,0:T(2,128)(2,1)} %all-gather.7.cloned.1.call-done), kind=kLoop, calls=%fused_computation.66 | loop fusion | bytes 6225920 | tf_op jit(solution)/shard_map/slice | solution.py:41
  142.6 50.8 %all-gather.5.cloned.1.call-done = bf16[2048,2560]{1,0:T(8,128)(2,1)} async-done(((bf16[64,2560]{1,0:T(8,128)(2,1)}), bf16[2048,2560]{1,0:T(8,128)(2,1)}) %all-gather.5.cloned.1.call-update) | async-done | bytes 10485776 | tf_op jit(solution)/shard_map/all_gather | solution.py:103
  193.4 9.8 %fusion.7 = f32[2048,304]{0,1:T(8,128)} fusion(bf16[2048,2560]{1,0:T(8,128)(2,1)} %all-gather.5.cloned.1.call-done, bf16[304,1,2560]{2,1,0:T(2,128)(2,1)} %get-tuple-element.15), kind=kOutput, calls=%fused_computation.16 | convolution fusion | flops 3187671040 | bytes 14532608 | tf_op jit(solution)/shard_map/td,fd->tf/dot_general | solution.py:40
  203.2 15.3 %convolution_convert_fusion = bf16[2048,2560]{1,0:T(8,128)(2,1)} fusion(bf16[304,2560]{1,0:T(8,128)(2,1)S(1)} %reshape.257, bf16[2048,2560]{1,0:T(8,128)(2,1)} %all-gather.5.cloned.1.call-done, f32[2048,304]{0,1:T(8,128)} %fusion.7, bf16[304,1,2560]{2,1,0:T(2,128)(2,1)} %get-tuple-element.14), kind=kOutput, calls=%fused_computation.1 | convolution fusion | flops 6384320512 | bytes 26574848 | tf_op jit(solution)/shard_map/dot_general | solution.py:43
  218.5 0.0 reduce-scatter.5.cloned.1.call-update
  218.5 1.0 slice.58
  219.6 0.1 copy_bitcast_fusion.6
  219.7 1.3 scatter_fusion
  221.0 0.9 copy.62
  221.9 94.3 %reduce-scatter.5.cloned.1.call-done = bf16[64,2560]{1,0:T(8,128)(2,1)} async-done(((bf16[2048,2560]{1,0:T(8,128)(2,1)}), bf16[64,2560]{1,0:T(8,128)(2,1)}) %reduce-scatter.5.cloned.1.call-update) | async-done | bytes 327696 | tf_op jit(solution)/shard_map/reduce_scatter | solution.py:105
  316.2 1.8 add_convert_fusion.1
  (25 shorter events, 0.1 us)
Async XLA Ops:
  7.2 56.6 %reduce-scatter.3.cloned.1.call-start = ((), (), s32[]{:S(2)}) async-start(), calls=%async_computation.2 | async-start | bytes 3276800 | tf_op jit(solution)/shard_map/reduce_scatter | solution.py:88
  14.8 1.1 copy-start.2
  14.8 1.4 copy-start.6
  16.2 2.1 copy-start.4
  16.6 2.9 copy-start.5
  21.2 2.3 slice-start
  21.2 2.6 slice-start.1
  26.9 36.9 %copy-start.1 = (bf16[256,2560]{1,0:T(8,128)(2,1)S(1)}, bf16[256,2560]{1,0:T(8,128)(2,1)}, u32[]{:S(2)}) copy-start(bf16[256,2560]{1,0:T(8,128)(2,1)} %param.11) | copy-start | bytes 3932164
  26.9 38.2 %copy-start.3 = (f32[2560]{0:T(1024)S(1)}, f32[2560]{0:T(1024)}, u32[]{:S(2)}) copy-start(f32[2560]{0:T(1024)} %param.19) | copy-start | bytes 30724
  26.9 65.3 %all-gather.9.cloned.1.call-start = ((), (), s32[]{:S(2)}) async-start(), calls=%async_computation.6 | async-start | bytes 2048000 | tf_op jit(solution)/shard_map/all_gather | solution.py:101
  27.6 105.5 %all-gather.7.cloned.1.call-start = ((), (), s32[]{:S(2)}) async-start(), calls=%async_computation.4 | async-start | bytes 3891200 | tf_op jit(solution)/shard_map/all_gather | solution.py:100
  28.4 165.0 %all-gather.5.cloned.1.call-start = ((), (), s32[]{:S(2)}) async-start(), calls=%async_computation.3 | async-start | bytes 10813440 | tf_op jit(solution)/shard_map/all_gather | solution.py:103
  67.0 249.2 %reduce-scatter.5.cloned.1.call-start = ((), (), s32[]{:S(2)}) async-start(), calls=%async_computation.5 | async-start | bytes 10813440 | tf_op jit(solution)/shard_map/reduce_scatter | solution.py:105
  218.5 1.2 copy-start.7
  218.5 97.7 %copy-start = (f32[64,2560]{1,0:T(8,128)S(1)}, f32[64,2560]{1,0:T(8,128)}, u32[]{:S(2)}) copy-start(f32[64,2560]{1,0:T(8,128)} %reduce-scatter.3.cloned.1.call-done) | copy-start | bytes 1966084
Sparse Core Ops, SparseCore 0:
  27.0 36.7 reduce-scatter.2
  65.4 26.7 all-gather.8
  93.9 39.1 all-gather.6
  135.8 57.5 all-gather.4
  218.6 97.5 reduce-scatter.4
where the time goes:
time: 325 us
  waiting for transfers between devices  246 us (76%)
  matrix products  36.6 us (11%)
  local copies, waits for them, and re-layouts  16.8 us (5%)
  between operations  14 us (4%)
  other arithmetic  10.5 us (3%)
    reduce_scatter x1, waiting for transfers between devices, per_device(): lax.psum_scatter(feed_forward(piece, unit_pairs, unit_down).astype(jnp.bf...  94.3 us
    all_gather x1, waiting for transfers between devices, per_device(): gathered = lax.all_gather(mlp_in, 'req', axis=0, tiled=True)  50.8 us
    all_gather x1, waiting for transfers between devices, per_device(): lax.all_gather(gate_up, 'mlp', axis=0, tiled=True)  39.3 us
    reduce_scatter x1, waiting for transfers between devices, per_device(): lax.psum_scatter(jnp.dot(piece, o_weight, preferred_element_type=jnp.floa...  35.3 us
    all_gather x1, waiting for transfers between devices, per_device(): lax.all_gather(down_weight, 'mlp', axis=0, tiled=True)  25 us
    dot_general x1, matrix products, feed_forward(): return jnp.dot(act, unit_down, preferred_element_type=jnp.float32)  15.3 us
    dot_general x1, matrix products, feed_forward(): jnp.einsum('td,fd->tf', rows, unit_pairs[:, 0, :], preferred_element_type...  9.78 us
    slice x1, local copies, waits for them, and re-layouts, feed_forward(): unit_pairs[:, 1, :]  9.43 us
  transfers between devices with their start and end apart: 5, of which 5 were waited for; matrix products, arithmetic and copies ran while one was open for 5% of the time, Pallas kernels for 0%

commit v1 on v0

--- a/solution.py
+++ b/solution.py
@@ -98,7 +98,9 @@
     mlp_in = rms_scale(resid, mlp_norm).astype(jnp.bfloat16)
     unit_pairs, unit_down = (
         lax.all_gather(gate_up, "mlp", axis=0, tiled=True),
-        lax.all_gather(down_weight, "mlp", axis=0, tiled=True),
+        jnp.concatenate(
+            lax.all_to_all(jnp.stack([down_weight] * lax.axis_size("mlp")), "mlp", 0, 0), axis=0
+        ),
     )
     gathered = lax.all_gather(mlp_in, "req", axis=0, tiled=True)
     piece = gathered

time: 325 us -> 308 us (0.948)
  waiting for transfers between devices: 246 us -> 192 us
  blocking collectives: 0 us -> 37.3 us
    all_to_all x0 -> x1, blocking collectives: none -> 37.3 us  [per_device(): lax.all_to_all(jnp.stack([down_weight] * lax.axis_size('mlp')), 'mlp', 0, 0)]
    all_gather x1, waiting for transfers between devices: 39.3 us -> 10.5 us  [per_device(): lax.all_gather(gate_up, 'mlp', axis=0, tiled=True)]
    all_gather x1 -> x0, waiting for transfers between devices: 25 us -> none  [per_device(): lax.all_gather(down_weight, 'mlp', axis=0, tiled=True)]
  transfers between devices with their start and end apart: 5 -> 4, of which waited for: 5 -> 4; matrix products, arithmetic and copies ran while one was open for 5% -> 6% of each run, Pallas kernels for 0% -> 0%
where the time goes in v1:
time: 308 us
  waiting for transfers between devices  192 us (62%)
  blocking collectives  37.3 us (12%)
  matrix products  36.8 us (12%)
  local copies, waits for them, and re-layouts  16.7 us (5%)
  between operations  14 us (5%)
  other arithmetic  10.5 us (3%)
    reduce_scatter x1, waiting for transfers between devices, per_device(): lax.psum_scatter(feed_forward(piece, unit_pairs, unit_down).astype(jnp.bf...  94.3 us
    all_gather x1, waiting for transfers between devices, per_device(): gathered = lax.all_gather(mlp_in, 'req', axis=0, tiled=True)  50.5 us
    all_to_all x1, blocking collectives, per_device(): lax.all_to_all(jnp.stack([down_weight] * lax.axis_size('mlp')), 'mlp', 0, 0)  37.3 us
    reduce_scatter x1, waiting for transfers between devices, per_device(): lax.psum_scatter(jnp.dot(piece, o_weight, preferred_element_type=jnp.floa...  36 us
    dot_general x1, matrix products, feed_forward(): return jnp.dot(act, unit_down, preferred_element_type=jnp.float32)  15.3 us
    all_gather x1, waiting for transfers between devices, per_device(): lax.all_gather(gate_up, 'mlp', axis=0, tiled=True)  10.5 us
    dot_general x1, matrix products, feed_forward(): jnp.einsum('td,fd->tf', rows, unit_pairs[:, 0, :], preferred_element_type...  9.9 us
    slice x1, local copies, waits for them, and re-layouts, feed_forward(): unit_pairs[:, 1, :]  9.43 us
  transfers between devices with their start and end apart: 4, of which 4 were waited for; matrix products, arithmetic and copies ran while one was open for 6% of the time, Pallas kernels for 0%

profile of v1, /device:TPU:0, one launch (start us, length us, event | category | flops | bytes accessed | tf_op | source)
XLA Modules:
  0.0 307.6 jit_solution(9309065574292001811)
XLA Ops:
  7.2 0.0 reduce-scatter.3.cloned.1.call-start
  7.2 1.7 fusion.3
  8.9 5.9 %fusion = f32[256,2,768]{2,0,1:T(8,128)S(1)} fusion(bf16[2560,2,768]{2,1,0:T(2,128)(2,1)} %param.15, bf16[256,2560]{1,0:T(8,128)(2,1)} %param.11, f32[2560]{0:T(1024)} %param.14, f32[256]{0:T(256)S(1)} %add_rsqrt_fusion.2), kind=kOutput, calls=%fused_computation.2 | convolution fusion | flops 2015887360 | bytes 10759168 | tf_op jit(solution)/shard_map/sd,dkc->skc/dot_general | solution.py:68
  14.8 0.1 multiply_reduce_fusion.2
  15.0 1.0 copy-done.2
  15.9 0.3 fusion.28
  16.2 0.0 copy-start.6
  16.2 0.2 reduce-window.8
  16.4 0.1 convert_reduce_fusion
  16.5 0.1 fusion.18
  16.6 0.4 reshape.251
  17.0 0.6 multiply_reduce_fusion
  17.6 0.1 copy.53
  17.8 0.5 multiply_cosine_fusion
  18.3 1.1 multiply_multiply_fusion
  19.4 0.2 subtract_convert_fusion.1
  19.6 0.3 fusion.12
  19.9 0.4 subtract_convert_fusion
  20.4 0.9 fusion.6
  21.2 0.0 slice-start
  21.2 1.7 convolution_convert_fusion.1
  23.0 0.5 slice-done
  23.5 0.3 slice-done.1
  23.8 3.1 fusion.30
  26.9 0.0 reduce-scatter.3.cloned.1.call-update
  26.9 0.0 all-gather.5.cloned.1.call-start
  26.9 0.7 all-gather.5.cloned.1.call-update
  27.6 0.0 all-gather.3.cloned.1.call-start
  27.7 36.0 %reduce-scatter.3.cloned.1.call-done = f32[64,2560]{1,0:T(8,128)} async-done(((f32[256,2560]{1,0:T(8,128)}), f32[64,2560]{1,0:T(8,128)}) %reduce-scatter.3.cloned.1.call-update) | async-done | bytes 655376 | tf_op jit(solution)/shard_map/reduce_scatter | solution.py:88
  63.7 1.3 multiply_reduce_fusion.1
  65.0 1.9 multiply_convert_fusion
  67.0 0.0 all-gather.3.cloned.1.call-update
  67.0 0.0 reduce-scatter.5.cloned.1.call-start
  67.1 0.1 stack.4
  67.2 37.3 %all_to_all.5 = bf16[4,76,2560]{2,1,0:T(8,128)(2,1)S(1)} all-to-all(bf16[4,76,2560]{2,1,0:T(8,128)(2,1)S(1)} %stack.4), channel_id=1, replica_groups=mesh['req'=32,'mlp'=4] {'mlp'}, dimensions={0} | all-to-all | bytes 3112960 | tf_op jit(solution)/shard_map/all_to_all | solution.py:102
  104.5 1.3 reshape.253
  105.8 10.5 %all-gather.5.cloned.1.call-done = bf16[304,2,2560]{2,1,0:T(2,128)(2,1)} async-done(((bf16[76,2,2560]{2,1,0:T(2,128)(2,1)}), bf16[304,2,2560]{2,1,0:T(2,128)(2,1)}) %all-gather.5.cloned.1.call-update) | async-done | bytes 3112976 | tf_op jit(solution)/shard_map/all_gather | solution.py:100
  116.4 9.4 %fusion.27 = (bf16[304,1,2560]{2,1,0:T(2,128)(2,1)}, bf16[304,1,2560]{2,1,0:T(2,128)(2,1)}) fusion(bf16[304,2,2560]{2,1,0:T(2,128)(2,1)} %all-gather.5.cloned.1.call-done), kind=kLoop, calls=%fused_computation.66 | loop fusion | bytes 6225920 | tf_op jit(solution)/shard_map/slice | solution.py:41
  125.8 50.5 %all-gather.3.cloned.1.call-done = bf16[2048,2560]{1,0:T(8,128)(2,1)} async-done(((bf16[64,2560]{1,0:T(8,128)(2,1)}), bf16[2048,2560]{1,0:T(8,128)(2,1)}) %all-gather.3.cloned.1.call-update) | async-done | bytes 10485776 | tf_op jit(solution)/shard_map/all_gather | solution.py:105
  176.3 9.9 %fusion.7 = f32[2048,304]{0,1:T(8,128)} fusion(bf16[2048,2560]{1,0:T(8,128)(2,1)} %all-gather.3.cloned.1.call-done, bf16[304,1,2560]{2,1,0:T(2,128)(2,1)} %get-tuple-element.15), kind=kOutput, calls=%fused_computation.16 | convolution fusion | flops 3187671040 | bytes 14532608 | tf_op jit(solution)/shard_map/td,fd->tf/dot_general | solution.py:40
  186.2 15.3 %convolution_convert_fusion = bf16[2048,2560]{1,0:T(8,128)(2,1)} fusion(bf16[304,2560]{1,0:T(8,128)(2,1)S(1)} %copy-done.3, bf16[2048,2560]{1,0:T(8,128)(2,1)} %all-gather.3.cloned.1.call-done, f32[2048,304]{0,1:T(8,128)} %fusion.7, bf16[304,1,2560]{2,1,0:T(2,128)(2,1)} %get-tuple-element.14), kind=kOutput, calls=%fused_computation.1 | convolution fusion | flops 6384320512 | bytes 26574848 | tf_op jit(solution)/shard_map/dot_general | solution.py:43
  201.5 0.0 reduce-scatter.5.cloned.1.call-update
  201.6 1.0 slice.58
  202.6 0.1 copy_bitcast_fusion.6
  202.8 1.3 scatter_fusion
  204.1 0.9 copy.62
  205.0 94.3 %reduce-scatter.5.cloned.1.call-done = bf16[64,2560]{1,0:T(8,128)(2,1)} async-done(((bf16[2048,2560]{1,0:T(8,128)(2,1)}), bf16[64,2560]{1,0:T(8,128)(2,1)}) %reduce-scatter.5.cloned.1.call-update) | async-done | bytes 327696 | tf_op jit(solution)/shard_map/reduce_scatter | solution.py:107
  299.2 1.8 add_convert_fusion.1
  (28 shorter events, 0.1 us)
Async XLA Ops:
  7.2 56.6 %reduce-scatter.3.cloned.1.call-start = ((), (), s32[]{:S(2)}) async-start(), calls=%async_computation.3 | async-start | bytes 3276800 | tf_op jit(solution)/shard_map/reduce_scatter | solution.py:88
  14.8 1.1 copy-start.2
  14.8 1.4 copy-start.8
  16.2 2.1 copy-start.6
  16.6 2.9 copy-start.7
  21.2 2.3 slice-start
  21.2 2.6 slice-start.1
  26.9 36.9 %copy-start.1 = (bf16[256,2560]{1,0:T(8,128)(2,1)S(1)}, bf16[256,2560]{1,0:T(8,128)(2,1)}, u32[]{:S(2)}) copy-start(bf16[256,2560]{1,0:T(8,128)(2,1)} %param.11) | copy-start | bytes 3932164
  26.9 38.2 %copy-start.5 = (f32[2560]{0:T(1024)S(1)}, f32[2560]{0:T(1024)}, u32[]{:S(2)}) copy-start(f32[2560]{0:T(1024)} %param.19) | copy-start | bytes 30724
  26.9 40.2 %copy-start.4 = (bf16[76,2560]{1,0:T(8,128)(2,1)S(1)}, bf16[76,2560]{1,0:T(8,128)(2,1)}, u32[]{:S(2)}) copy-start(bf16[76,2560]{1,0:T(8,128)(2,1)} %param.21) | copy-start | bytes 1167364
  26.9 89.5 %all-gather.5.cloned.1.call-start = ((), (), s32[]{:S(2)}) async-start(), calls=%async_computation.5 | async-start | bytes 3891200 | tf_op jit(solution)/shard_map/all_gather | solution.py:100
  27.6 148.7 %all-gather.3.cloned.1.call-start = ((), (), s32[]{:S(2)}) async-start(), calls=%async_computation.4 | async-start | bytes 10813440 | tf_op jit(solution)/shard_map/all_gather | solution.py:105
  67.0 232.2 %reduce-scatter.5.cloned.1.call-start = ((), (), s32[]{:S(2)}) async-start(), calls=%async_computation.6 | async-start | bytes 10813440 | tf_op jit(solution)/shard_map/reduce_scatter | solution.py:107
  176.3 9.9 %copy-start.3 = (bf16[304,2560]{1,0:T(8,128)(2,1)S(1)}, bf16[304,2560]{1,0:T(8,128)(2,1)}, u32[]{:S(2)}) copy-start(bf16[304,2560]{1,0:T(8,128)(2,1)} %reshape.253) | copy-start | bytes 4669444
  201.5 1.2 copy-start.9
  201.5 97.7 %copy-start = (f32[64,2560]{1,0:T(8,128)S(1)}, f32[64,2560]{1,0:T(8,128)}, u32[]{:S(2)}) copy-start(f32[64,2560]{1,0:T(8,128)} %reduce-scatter.3.cloned.1.call-done) | copy-start | bytes 1966084
Sparse Core Ops, SparseCore 0:
  27.0 36.6 reduce-scatter.2
  65.4 50.9 all-gather.4
  119.2 57.0 all-gather.2
  201.7 97.5 reduce-scatter.4
